TPU v7x, 32 devices: a whole 2x2x4 slice. The times are simulated.
32 devices in a mesh: group: 4 (over x, core), replica: 8 (over z, y).
Axes of the slice: x: 2, y: 2, z: 4, core: 2. Of those that a mesh axis runs over, the one named last changes fastest.
Arguments:
- hidden_in: bfloat16 [8, 1024, 896], P('replica', 'group'), may hold values from -6 to 6
- out_grad: bfloat16 [8, 1024, 896], P('replica', 'group'), may hold values from -6 to 6
- positions: int32 [8, 1024], P('replica', 'group'), may hold values from 0 to 3069, as said below
- block_ids: int32 [8, 1024], P('replica'), may hold values from 0 to 7, never falling along the last dimension, each value on 1 to 256 neighbouring positions
- gain_one: bfloat16 [896], P('group'), may hold values from 0.5 to 1.5
- w_query: bfloat16 [896, 896], P('group'), may hold values from -0.1875 to 0.1875
- b_query: bfloat16 [896], P('group'), may hold values from -3 to 3
- w_key: bfloat16 [896, 128], P('group'), may hold values from -0.1875 to 0.1875
- b_key: bfloat16 [128], P('group'), may hold values from -3 to 3
- w_value: bfloat16 [896, 128], P('group'), may hold values from -0.1875 to 0.1875
- b_value: bfloat16 [128], P('group'), may hold values from -3 to 3
- w_out: bfloat16 [896, 896], P('group'), may hold values from -1.5 to 1.5
- gain_two: bfloat16 [896], P('group'), may hold values from 0.5 to 1.5
- w_gate: bfloat16 [896, 4864], P('group'), may hold values from -0.1875 to 0.1875
- w_up: bfloat16 [896, 4864], P('group'), may hold values from -0.1875 to 0.1875
- w_down: bfloat16 [4864, 896], P('group'), may hold values from -0.078125 to 0.078125
Outputs:
- layer_out: bfloat16 [8, 1024, 896], P('replica', 'group')
- in_grad: bfloat16 [8, 1024, 896], P('replica', 'group')
- grad_gain_one: float32 [896], P('group')
- grad_w_query: float32 [896, 896], P('group')
- grad_b_query: float32 [896], P('group')
- grad_w_key: float32 [896, 128], P('group')
- grad_b_key: float32 [128], P('group')
- grad_w_value: float32 [896, 128], P('group')
- grad_b_value: float32 [128], P('group')
- grad_w_out: float32 [896, 896], P('group')
- grad_gain_two: float32 [896], P('group')
- grad_w_gate: float32 [896, 4864], P('group')
- grad_w_up: float32 [896, 4864], P('group')
- grad_w_down: float32 [4864, 896], P('group')
Inputs may be any that keep to these rules, and one draw needn't show every extreme that they name: `block_ids`: along each sequence block ids never fall, and one block holds at most 256 tokens. Each sequence starts at position 0, and positions rise by 1, 2 or 3 from token to token.
All inputs are finite; a program needn't handle non-finite values.
Results may differ from a plain program's by a relative error of at most 0.018.
Values may be sent and summed in bfloat16 or wider, within the bound.
No kernel may reach another device: no remote copies, remote signals or barrier semaphores. Data moves between devices by JAX's collectives and lax.ppermute only.
A program may use at most 256 MiB of HBM per device.

v0:
```python
import jax
import jax.numpy as jnp
from jax import lax
from jax.sharding import PartitionSpec as P

HEADS = 14
KV_HEADS = 2
HEAD_DIM = 64
EPSILON = 1e-06
THETA = 1000000.0


def rms_scale(values):
    return lax.rsqrt(jnp.mean(values * values, axis=-1, keepdims=True) + EPSILON)


def rotate(values, cosine, sine):
    half = values.shape[-1] // 2
    turned = jnp.concatenate([-values[..., half:], values[..., :half]], axis=-1)
    return values * cosine + turned * sine


def norm_back(grad_normed, unit, scale, gain):
    grad_gain = jnp.sum(grad_normed * unit, axis=(0, 1))
    inner = grad_normed * gain
    grad_in = scale * (inner - unit * jnp.mean(inner * unit, axis=-1, keepdims=True))
    return (grad_gain, grad_in)


def project(left, right):
    return jnp.einsum("bpd,de->bpe", left, right, preferred_element_type=jnp.float32)


def project_back(left, right):
    return jnp.einsum("bpe,de->bpd", left, right, preferred_element_type=jnp.float32)


def weight_grad(left, right):
    return jnp.einsum("bpd,bpe->de", left, right, preferred_element_type=jnp.float32)


def body(
    hidden_in,
    out_grad,
    positions,
    block_ids,
    gain_one,
    w_query,
    b_query,
    w_key,
    b_key,
    w_value,
    b_value,
    w_out,
    gain_two,
    w_gate,
    w_up,
    w_down,
):
    f32 = jnp.float32
    bf16 = jnp.bfloat16
    batch, part, width = hidden_in.shape
    length = block_ids.shape[1]
    head_dim = HEAD_DIM
    kv_heads = KV_HEADS
    groups = HEADS // KV_HEADS
    factor = 1.0 / head_dim**0.5
    attn_full = (
        lax.all_gather(gain_one, "group", axis=0, tiled=True),
        lax.all_gather(w_query, "group", axis=0, tiled=True),
        lax.all_gather(b_query, "group", axis=0, tiled=True),
        lax.all_gather(w_key, "group", axis=0, tiled=True),
        lax.all_gather(b_key, "group", axis=0, tiled=True),
        lax.all_gather(w_value, "group", axis=0, tiled=True),
        lax.all_gather(b_value, "group", axis=0, tiled=True),
        lax.all_gather(w_out, "group", axis=0, tiled=True),
    )
    mlp_full = (
        lax.all_gather(gain_two, "group", axis=0, tiled=True),
        lax.all_gather(w_gate, "group", axis=0, tiled=True),
        lax.all_gather(w_up, "group", axis=0, tiled=True),
        lax.all_gather(w_down, "group", axis=0, tiled=True),
    )
    g_one, wq_full, bq_full, wk_full, bk_full, wv_full, bv_full, wo_full = attn_full
    g_two, wg_full, wu_full, wd_full = mlp_full
    half = head_dim // 2
    freqs = THETA ** (-(2.0 * jnp.arange(half, dtype=f32)) / head_dim)
    angles = positions.astype(f32)[..., None] * freqs
    angles = jnp.concatenate([angles, angles], axis=-1)[:, :, None, :]
    cosine = jnp.cos(angles)
    sine = jnp.sin(angles)
    x_value = hidden_in.astype(f32)
    scale_one = rms_scale(x_value)
    unit_one = x_value * scale_one
    gain_first = g_one.astype(f32)
    normed_one = (unit_one * gain_first).astype(bf16)
    query_pre = project(normed_one, wq_full) + bq_full.astype(f32)
    key_pre = project(normed_one, wk_full) + bk_full.astype(f32)
    value_low = (project(normed_one, wv_full) + bv_full.astype(f32)).astype(bf16)
    query = rotate(query_pre.reshape(batch, part, HEADS, head_dim), cosine, sine).astype(bf16)
    key_low = rotate(key_pre.reshape(batch, part, kv_heads, head_dim), cosine, sine).astype(bf16)
    key_low = key_low.reshape(batch, part, kv_heads * head_dim)
    keys_all, values_all = (
        lax.all_gather(key_low, "group", axis=1, tiled=True),
        lax.all_gather(value_low, "group", axis=1, tiled=True),
    )
    key_heads = keys_all.reshape(batch, length, kv_heads, head_dim)
    value_heads = values_all.reshape(batch, length, kv_heads, head_dim)
    query_heads = query.reshape(batch, part, kv_heads, groups, head_dim)
    start = lax.axis_index("group") * part
    query_blocks = lax.dynamic_slice_in_dim(block_ids, start, part, 1)
    visible = (block_ids[:, None, :] <= query_blocks[:, :, None])[:, None, None, :, :]
    scores = (
        jnp.einsum("bqgha,bkga->bghqk", query_heads, key_heads, preferred_element_type=f32) * factor
    )
    masked = jnp.where(visible, scores, -jnp.inf)
    top = jnp.max(masked, axis=-1, keepdims=True)
    raised = jnp.exp(masked - top)
    total = jnp.sum(raised, axis=-1, keepdims=True)
    log_total = top + jnp.log(total)
    probs_low = (raised / total).astype(bf16)
    attended = jnp.einsum("bghqk,bkga->bqgha", probs_low, value_heads, preferred_element_type=f32)
    attended = attended.reshape(batch, part, HEADS * head_dim).astype(bf16)
    residual = x_value + project(attended, wo_full)
    scale_two = rms_scale(residual)
    unit_two = residual * scale_two
    gain_second = g_two.astype(f32)
    normed_two = (unit_two * gain_second).astype(bf16)
    gate = project(normed_two, wg_full)
    up_value = project(normed_two, wu_full)
    sigma = jax.nn.sigmoid(gate)
    activated = gate * sigma
    hidden = (activated * up_value).astype(bf16)
    layer_out = (residual + project(hidden, wd_full)).astype(bf16)
    g_two_b, wg_back, wu_back, wd_back = (
        lax.all_gather(gain_two, "group", axis=0, tiled=True),
        lax.all_gather(w_gate, "group", axis=0, tiled=True),
        lax.all_gather(w_up, "group", axis=0, tiled=True),
        lax.all_gather(w_down, "group", axis=0, tiled=True),
    )
    g_one_b, wq_back, wk_back, wv_back, wo_back = (
        lax.all_gather(gain_one, "group", axis=0, tiled=True),
        lax.all_gather(w_query, "group", axis=0, tiled=True),
        lax.all_gather(w_key, "group", axis=0, tiled=True),
        lax.all_gather(w_value, "group", axis=0, tiled=True),
        lax.all_gather(w_out, "group", axis=0, tiled=True),
    )
    grad_out = out_grad.astype(f32)
    grad_down = weight_grad(hidden, out_grad)
    grad_hidden = project_back(out_grad, wd_back)
    grad_gate_pre = (grad_hidden * up_value * sigma * (1.0 + gate * (1.0 - sigma))).astype(bf16)
    grad_up_pre = (grad_hidden * activated).astype(bf16)
    grad_gate = weight_grad(normed_two, grad_gate_pre)
    grad_up = weight_grad(normed_two, grad_up_pre)
    grad_normed_two = project_back(grad_gate_pre, wg_back) + project_back(grad_up_pre, wu_back)
    grad_gain_two, grad_res_norm = norm_back(
        grad_normed_two, unit_two, scale_two, g_two_b.astype(f32)
    )
    grad_residual = grad_out + grad_res_norm
    grad_branch = grad_residual.astype(bf16)
    grad_wo = weight_grad(attended, grad_branch)
    grad_attended = project_back(grad_branch, wo_back).astype(bf16)
    grad_att_heads = grad_attended.reshape(batch, part, kv_heads, groups, head_dim)
    again = (
        jnp.einsum("bqgha,bkga->bghqk", query_heads, key_heads, preferred_element_type=f32) * factor
    )
    probs = jnp.where(visible, jnp.exp(again - log_total), 0.0)
    probs_back = probs.astype(bf16)
    grad_probs = jnp.einsum(
        "bqgha,bkga->bghqk", grad_att_heads, value_heads, preferred_element_type=f32
    )
    grad_values_all = jnp.einsum(
        "bghqk,bqgha->bkga", probs_back, grad_att_heads, preferred_element_type=f32
    )
    row_sum = jnp.sum(probs * grad_probs, axis=-1, keepdims=True)
    grad_scores = (probs * (grad_probs - row_sum)).astype(bf16)
    grad_query = (
        jnp.einsum("bghqk,bkga->bqgha", grad_scores, key_heads, preferred_element_type=f32) * factor
    )
    grad_keys_all = (
        jnp.einsum("bghqk,bqgha->bkga", grad_scores, query_heads, preferred_element_type=f32)
        * factor
    )
    grad_key_local, grad_value_local = (
        lax.psum_scatter(
            grad_keys_all.reshape(batch, length, kv_heads * head_dim),
            "group",
            scatter_dimension=1,
            tiled=True,
        ),
        lax.psum_scatter(
            grad_values_all.reshape(batch, length, kv_heads * head_dim),
            "group",
            scatter_dimension=1,
            tiled=True,
        ),
    )
    grad_query_pre = rotate(grad_query.reshape(batch, part, HEADS, head_dim), cosine, -sine).astype(
        bf16
    )
    grad_query_pre = grad_query_pre.reshape(batch, part, HEADS * head_dim)
    grad_key_pre = rotate(
        grad_key_local.reshape(batch, part, kv_heads, head_dim), cosine, -sine
    ).astype(bf16)
    grad_key_pre = grad_key_pre.reshape(batch, part, kv_heads * head_dim)
    grad_value_pre = grad_value_local.astype(bf16)
    grad_bq = jnp.sum(grad_query_pre.astype(f32), axis=(0, 1))
    grad_bk = jnp.sum(grad_key_pre.astype(f32), axis=(0, 1))
    grad_bv = jnp.sum(grad_value_pre.astype(f32), axis=(0, 1))
    grad_wq = weight_grad(normed_one, grad_query_pre)
    grad_wk = weight_grad(normed_one, grad_key_pre)
    grad_wv = weight_grad(normed_one, grad_value_pre)
    grad_normed_one = (
        project_back(grad_query_pre, wq_back)
        + project_back(grad_key_pre, wk_back)
        + project_back(grad_value_pre, wv_back)
    )
    grad_gain_one, grad_in_norm = norm_back(
        grad_normed_one, unit_one, scale_one, g_one_b.astype(f32)
    )
    in_grad = (grad_residual + grad_in_norm).astype(bf16)
    shards = (
        lax.psum_scatter(grad_gain_one, "group", scatter_dimension=0, tiled=True),
        lax.psum_scatter(grad_wq, "group", scatter_dimension=0, tiled=True),
        lax.psum_scatter(grad_bq, "group", scatter_dimension=0, tiled=True),
        lax.psum_scatter(grad_wk, "group", scatter_dimension=0, tiled=True),
        lax.psum_scatter(grad_bk, "group", scatter_dimension=0, tiled=True),
        lax.psum_scatter(grad_wv, "group", scatter_dimension=0, tiled=True),
        lax.psum_scatter(grad_bv, "group", scatter_dimension=0, tiled=True),
        lax.psum_scatter(grad_wo, "group", scatter_dimension=0, tiled=True),
        lax.psum_scatter(grad_gain_two, "group", scatter_dimension=0, tiled=True),
        lax.psum_scatter(grad_gate, "group", scatter_dimension=0, tiled=True),
        lax.psum_scatter(grad_up, "group", scatter_dimension=0, tiled=True),
        lax.psum_scatter(grad_down, "group", scatter_dimension=0, tiled=True),
    )
    shards = lax.psum(tuple(shards), "replica")
    return (layer_out, in_grad) + tuple(shards)


def solution(mesh):
    in_specs = (
        P("replica", "group", None),
        P("replica", "group", None),
        P("replica", "group"),
        P("replica", None),
        P("group"),
        P("group", None),
        P("group"),
        P("group", None),
        P("group"),
        P("group", None),
        P("group"),
        P("group", None),
        P("group"),
        P("group", None),
        P("group", None),
        P("group", None),
    )
    out_specs = (
        P("replica", "group", None),
        P("replica", "group", None),
        P("group"),
        P("group", None),
        P("group"),
        P("group", None),
        P("group"),
        P("group", None),
        P("group"),
        P("group", None),
        P("group"),
        P("group", None),
        P("group", None),
        P("group", None),
    )
    return jax.shard_map(body, mesh=mesh, in_specs=in_specs, out_specs=out_specs, check_vma=False)
```

profile of v0, /device:TPU:0, one launch (start us, length us, event | category | flops | bytes accessed | tf_op | source)
XLA Modules:
  0.0 1366.9 jit_solution(3879339385631987859)
XLA Ops:
  7.3 0.7 all-gather.8.cloned.1.call-update
  8.1 0.7 all-gather.10.cloned.1.call-update
  13.9 8.5 all-reduce.13
  22.4 6.9 all_gather.52
  30.4 5.9 all-gather
  36.2 0.8 copy.49
  37.7 5.7 all_gather.55
  44.7 7.7 all-gather.1
  52.6 2.2 convolution_add_fusion.2
  55.4 7.4 fusion.5
  62.8 10.3 fusion.6
  73.1 7.9 fusion.22
  81.0 2.4 multiply_reduce_fusion
  83.6 34.6 %all-gather.12.cloned.1.call-done = bf16[896,4864]{1,0:T(8,128)(2,1)} async-done(((bf16[224,4864]{1,0:T(8,128)(2,1)}), bf16[896,4864]{1,0:T(8,128)(2,1)}) %all-gather.12.cloned.1.call-update) | async-done | bytes 8716304 | tf_op jit(solution)/shard_map/all_gather | solution.py:80
  118.2 7.9 fusion.86
  126.1 53.7 %all-gather.14.cloned.1.call-done = bf16[896,4864]{1,0:T(8,128)(2,1)} async-done(((bf16[224,4864]{1,0:T(8,128)(2,1)}), bf16[896,4864]{1,0:T(8,128)(2,1)}) %all-gather.14.cloned.1.call-update) | async-done | bytes 8716304 | tf_op jit(solution)/shard_map/all_gather | solution.py:81
  179.8 7.9 fusion.87
  187.7 53.8 %all-gather.16.cloned.1.call-done = bf16[4864,896]{1,0:T(8,128)(2,1)} async-done(((bf16[1216,896]{1,0:T(8,128)(2,1)}), bf16[4864,896]{1,0:T(8,128)(2,1)}) %all-gather.16.cloned.1.call-update) | async-done | bytes 8716304 | tf_op jit(solution)/shard_map/all_gather | solution.py:82
  241.4 11.3 multiply_convert_fusion
  252.7 8.0 fusion.88
  260.9 3.5 fusion.39
  264.6 0.7 convolution_convert_fusion
  265.7 12.5 fusion
  278.2 1.5 slice-done.2
  280.2 7.6 fusion.9
  287.9 3.0 copy-done
  290.8 3.1 fusion.25
  294.0 7.5 fusion.12
  301.6 0.8 broadcast_multiply_fusion.1
  302.4 13.3 reduce-scatter.10.cloned.1.call-done
  315.7 0.9 slice_negate_fusion.2
  316.6 1.0 convert_reduce_fusion.2
  317.7 1.2 fusion.67
  319.2 5.4 broadcast_multiply_fusion
  324.6 16.0 %reduce-scatter.12.cloned.1.call-done = f32[1,256,128]{1,2,0:T(8,128)} async-done(((f32[1,1024,128]{1,2,0:T(8,128)}), f32[1,256,128]{1,2,0:T(8,128)}) %reduce-scatter.12.cloned.1.call-update) | async-done | bytes 131088 | tf_op jit(solution)/shard_map/reduce_scatter | solution.py:191
  340.6 2.1 fusion.64
  342.9 0.9 copy-done.3
  343.8 1.5 add_convert_fusion
  345.3 2.5 fusion.79
  347.9 2.3 fusion.47
  350.3 10.3 fusion.90
  360.6 10.1 fusion.91
  370.8 0.9 copy-done.15
  371.8 10.5 fusion.50
  382.7 6.6 reduce-scatter.18.cloned.1.call-done
  389.3 41.4 %reduce-scatter.14.cloned.1.call-done = f32[224,896]{1,0:T(8,128)} async-done(((f32[896,896]{1,0:T(8,128)}), f32[224,896]{1,0:T(8,128)}) %reduce-scatter.14.cloned.1.call-update) | async-done | bytes 802832 | tf_op jit(solution)/shard_map/reduce_scatter | solution.py:224
  430.6 41.7 %reduce-scatter.20.cloned.1.call-done = f32[224,896]{1,0:T(8,128)} async-done(((f32[896,896]{1,0:T(8,128)}), f32[224,896]{1,0:T(8,128)}) %reduce-scatter.20.cloned.1.call-update) | async-done | bytes 802832 | tf_op jit(solution)/shard_map/reduce_scatter | solution.py:230
  472.3 132.6 %reduce-scatter.22.cloned.1.call-done = f32[224,4864]{1,0:T(8,128)} async-done(((f32[896,4864]{1,0:T(8,128)}), f32[224,4864]{1,0:T(8,128)}) %reduce-scatter.22.cloned.1.call-update) | async-done | bytes 4358160 | tf_op jit(solution)/shard_map/reduce_scatter | solution.py:232
  604.9 132.9 %reduce-scatter.24.cloned.1.call-done = f32[224,4864]{1,0:T(8,128)} async-done(((f32[896,4864]{1,0:T(8,128)}), f32[224,4864]{1,0:T(8,128)}) %reduce-scatter.24.cloned.1.call-update) | async-done | bytes 4358160 | tf_op jit(solution)/shard_map/reduce_scatter | solution.py:233
  737.9 132.6 %reduce-scatter.26.cloned.1.call-done = f32[1216,896]{1,0:T(8,128)} async-done(((f32[4864,896]{1,0:T(8,128)}), f32[1216,896]{1,0:T(8,128)}) %reduce-scatter.26.cloned.1.call-update) | async-done | bytes 4358160 | tf_op jit(solution)/shard_map/reduce_scatter | solution.py:234
  871.8 1.3 fusion.41
  873.2 2.2 fusion.89
  875.4 7.9 fusion.21
  884.3 10.9 all-reduce.12
  895.6 23.2 %all-reduce.10 = (f32[224]{0:T(256)}, f32[224]{0:T(256)}, f32[32]{0:T(128)}, f32[32]{0:T(128)}, f32[224]{0:T(256)}) all-reduce(f32[224]{0:T(256)S(1)} %dynamic-slice.6, f32[224]{0:T(256)S(1)} %dynamic-slice.8, f32[32]{0:T(128)S(1)} %dynamic-slice.10, f32[32]{0:T(128)S(1)} %dynamic-slice.12, ...), channel_id=1, replica_groups=mesh['group'=4,'replica'=8] {'replica'}, use_global_device_ids=true, to_apply=%region_11.12 | all-reduce | flops 736 | bytes 5888 | tf_op jit(solution)/shard_map/psum | solution.py:236
  918.9 1.1 fusion.32
  919.9 423.7 %all-reduce.16.cloned.1.call-done = (f32[224,896]{1,0:T(8,128)}, f32[224,128]{1,0:T(8,128)}, f32[224,128]{1,0:T(8,128)}, f32[224,896]{1,0:T(8,128)}, f32[224,486...) async-done(((f32[224,896]{1,0:T(8,128)}, f32[224,128]{1,0:T(8,128)}, f32[224,128]{1,0:T(8,128)}, f32[224,896]{1,0:T(8,128)}, f32[224,4864]{1,0:T(8,128)}, ...) | async-done | bytes 14909456 | tf_op jit(solution)/shard_map/psum | solution.py:236
  1343.6 2.2 copy.77
  1345.8 1.6 copy.78
  1347.4 1.6 copy.79
  1348.9 2.1 copy.80
  1351.0 4.7 copy.81
  1355.8 2.1 copy.82
  1357.8 2.1 copy.83
  (184 shorter events, 11.5 us)
Async XLA Ops:
  7.2 3.6 copy-start.39
  7.2 5.5 copy-start.41
  7.2 5.7 copy-start.42
  7.2 5.9 copy-start.43
  7.2 6.2 copy-start.44
  7.2 6.4 copy-start.45
  7.2 15.1 %copy-start.28 = (bf16[224,128]{1,0:T(8,128)(2,1)S(1)}, bf16[224,128]{1,0:T(8,128)(2,1)}, u32[]{:S(2)}) copy-start(bf16[224,128]{1,0:T(8,128)(2,1)} %param.25) | copy-start | bytes 172036
  7.3 22.1 %copy-start.1 = (bf16[1,256,896]{2,1,0:T(8,128)(2,1)S(1)}, bf16[1,256,896]{2,1,0:T(8,128)(2,1)}, u32[]{:S(2)}) copy-start(bf16[1,256,896]{2,1,0:T(8,128)(2,1)} %param.16) | copy-start | bytes 1376260
  7.3 29.8 %copy-start.40 = (s32[1,256]{1,0:T(1,128)S(1)}, s32[1,256]{1,0:T(1,128)}, u32[]{:S(2)}) copy-start(s32[1,256]{1,0:T(1,128)} %param.18) | copy-start | bytes 3076
  7.3 30.4 %copy-start.29 = (bf16[224,128]{1,0:T(8,128)(2,1)S(1)}, bf16[224,128]{1,0:T(8,128)(2,1)}, u32[]{:S(2)}) copy-start(bf16[224,128]{1,0:T(8,128)(2,1)} %param.23) | copy-start | bytes 172036
  7.3 45.1 %copy-start.37 = (s32[1,1024]{1,0:T(1,128)S(1)}, s32[1,1024]{1,0:T(1,128)}, u32[]{:S(2)}) copy-start(s32[1,1024]{1,0:T(1,128)} %param.19) | copy-start | bytes 12292
  7.3 45.3 %all-gather.8.cloned.1.call-start = ((), (), s32[]{:S(2)}) async-start(), calls=%async_computation.9 | async-start | bytes 2007040 | tf_op jit(solution)/shard_map/all_gather | solution.py:70
  8.0 73.0 %all-gather.10.cloned.1.call-start = ((), (), s32[]{:S(2)}) async-start(), calls=%async_computation.10 | async-start | bytes 2007040 | tf_op jit(solution)/shard_map/all_gather | solution.py:76
  8.8 109.4 %all-gather.12.cloned.1.call-start = ((), (), s32[]{:S(2)}) async-start(), calls=%async_computation.11 | async-start | bytes 10895360 | tf_op jit(solution)/shard_map/all_gather | solution.py:80
  9.5 170.2 %all-gather.14.cloned.1.call-start = ((), (), s32[]{:S(2)}) async-start(), calls=%async_computation.12 | async-start | bytes 10895360 | tf_op jit(solution)/shard_map/all_gather | solution.py:81
  10.1 231.3 %all-gather.16.cloned.1.call-start = ((), (), s32[]{:S(2)}) async-start(), calls=%async_computation.13 | async-start | bytes 10895360 | tf_op jit(solution)/shard_map/all_gather | solution.py:82
  10.7 305.0 %reduce-scatter.10.cloned.1.call-start = ((), (), s32[]{:S(2)}) async-start(), calls=%async_computation.14 | async-start | bytes 655360 | tf_op jit(solution)/shard_map/reduce_scatter | solution.py:185
  22.4 30.2 %copy-start.25 = (f32[896]{0:T(1024)}, f32[896]{0:T(1024)S(1)}, u32[]{:S(2)}) copy-start(f32[896]{0:T(1024)S(1)} %convert_element_type.154) | copy-start | bytes 10756
  30.0 22.6 %copy-start.32 = (f32[256]{0:T(256)}, f32[256]{0:T(256)S(1)}, u32[]{:S(2)}) copy-start(f32[256]{0:T(256)S(1)} %add_rsqrt_fusion.1) | copy-start | bytes 3076
  43.4 9.3 copy-start.20
  52.3 10.4 copy-start.9
  62.8 10.3 copy-start.17
  73.1 10.4 copy-start.30
  81.0 45.1 %copy-start.11 = (bf16[2,64,7,256]{3,1,2,0:T(8,128)(2,1)}, bf16[2,64,7,256]{3,1,2,0:T(8,128)(2,1)S(1)}, u32[]{:S(2)}) copy-start(bf16[2,64,7,256]{3,1,2,0:T(8,128)(2,1)S(1)} %fusion.22) | copy-start | bytes 1376260
  83.4 181.0 %copy-start.4 = (f32[1,256,896]{2,1,0:T(8,128)}, f32[1,256,896]{2,1,0:T(8,128)S(1)}, u32[]{:S(2)}) copy-start(f32[1,256,896]{2,1,0:T(8,128)S(1)} %get-tuple-element.64) | copy-start | bytes 2752516
  83.4 34.8 %copy-start.35 = (f32[256]{0:T(256)}, f32[256]{0:T(256)S(1)}, u32[]{:S(2)}) copy-start(f32[256]{0:T(256)S(1)} %add_rsqrt_fusion) | copy-start | bytes 3076
  126.1 115.3 %copy-start.13 = (bf16[1,256,896]{2,1,0:T(8,128)(2,1)S(1)}, bf16[1,256,896]{2,1,0:T(8,128)(2,1)}, u32[]{:S(2)}) copy-start(bf16[1,256,896]{2,1,0:T(8,128)(2,1)} %param.17) | copy-start | bytes 1376260
  252.7 8.1 copy-start.8
  252.7 8.1 copy-start.7
  252.7 8.1 copy-start.2
  252.7 8.1 copy-start.31
  252.7 8.1 copy-start.36
  260.8 3.5 copy-start.14
  260.9 3.8 copy-start.5
  265.6 12.5 slice-start
  265.6 12.5 slice-start.1
  265.6 14.0 %slice-start.2 = ((s8[14680064]{0:T(1024)(128)(4,1)}), s8[4194304]{0:T(1024)(128)(4,1)S(1)}, s32[]{:S(2)}) async-start(s8[14680064]{0:T(1024)(128)(4,1)} %bitcast.259), calls=%async_computation.26 | async-start | bytes 8388608
  265.6 14.6 %slice-start.3 = ((s8[14680064]{0:T(1024)(128)(4,1)}), s8[2097152]{0:T(1024)(128)(4,1)S(1)}, s32[]{:S(2)}) async-start(s8[14680064]{0:T(1024)(128)(4,1)} %bitcast.259), calls=%async_computation.27 | async-start | bytes 4194304
  287.8 3.0 copy-start
  293.9 7.7 copy-start.23
  294.0 23.7 %copy-start.26 = (f32[896]{0:T(1024)S(1)}, f32[896]{0:T(1024)}, u32[]{:S(2)}) copy-start(f32[896]{0:T(1024)} %copy-done.25) | copy-start | bytes 10756
  294.0 23.7 %copy-start.33 = (f32[256]{0:T(256)S(1)}, f32[256]{0:T(256)}, u32[]{:S(2)}) copy-start(f32[256]{0:T(256)} %copy-done.32) | copy-start | bytes 3076
  294.0 25.2 %copy-start.10 = (bf16[1024,128]{0,1:T(8,128)(2,1)S(1)}, bf16[1024,128]{0,1:T(8,128)(2,1)}, u32[]{:S(2)}) copy-start(bf16[1024,128]{0,1:T(8,128)(2,1)} %copy-done.9) | copy-start | bytes 786436
  294.0 46.6 %reduce-scatter.12.cloned.1.call-start = ((), (), s32[]{:S(2)}) async-start(), calls=%async_computation.15 | async-start | bytes 655360 | tf_op jit(solution)/shard_map/reduce_scatter | solution.py:191
  301.5 81.1 %reduce-scatter.16.cloned.1.call-start = ((), (), s32[]{:S(2)}) async-start(), calls=%async_computation.17 | async-start | bytes 573440 | tf_op jit(solution)/shard_map/reduce_scatter | solution.py:226
  318.9 24.9 %copy-start.24 = (f32[256,64]{0,1:T(8,128)S(1)}, f32[256,64]{0,1:T(8,128)}, u32[]{:S(2)}) copy-start(f32[256,64]{0,1:T(8,128)} %get-tuple-element.55) | copy-start | bytes 196612
  318.9 26.4 %copy-start.27 = (f32[896]{0:T(1024)S(1)}, f32[896]{0:T(1024)}, u32[]{:S(2)}) copy-start(f32[896]{0:T(1024)} %copy-done.25) | copy-start | bytes 10756
  318.9 26.4 %copy-start.34 = (f32[256]{0:T(256)S(1)}, f32[256]{0:T(256)}, u32[]{:S(2)}) copy-start(f32[256]{0:T(256)} %copy-done.32) | copy-start | bytes 3076
  318.9 70.3 %reduce-scatter.18.cloned.1.call-start = ((), (), s32[]{:S(2)}) async-start(), calls=%async_computation.18 | async-start | bytes 573440 | tf_op jit(solution)/shard_map/reduce_scatter | solution.py:228
  342.7 5.2 copy-start.12
  342.7 87.9 %reduce-scatter.14.cloned.1.call-start = ((), (), s32[]{:S(2)}) async-start(), calls=%async_computation.16 | async-start | bytes 4014080 | tf_op jit(solution)/shard_map/reduce_scatter | solution.py:224
  347.8 124.5 %reduce-scatter.20.cloned.1.call-start = ((), (), s32[]{:S(2)}) async-start(), calls=%async_computation.19 | async-start | bytes 4014080 | tf_op jit(solution)/shard_map/reduce_scatter | solution.py:230
  350.2 254.7 %reduce-scatter.22.cloned.1.call-start = ((), (), s32[]{:S(2)}) async-start(), calls=%async_computation.20 | async-start | bytes 21790720 | tf_op jit(solution)/shard_map/reduce_scatter | solution.py:232
  360.6 377.3 %reduce-scatter.24.cloned.1.call-start = ((), (), s32[]{:S(2)}) async-start(), calls=%async_computation.21 | async-start | bytes 21790720 | tf_op jit(solution)/shard_map/reduce_scatter | solution.py:233
  370.8 1.0 copy-start.15
  370.8 499.7 %reduce-scatter.26.cloned.1.call-start = ((), (), s32[]{:S(2)}) async-start(), calls=%async_computation.22 | async-start | bytes 21790720 | tf_op jit(solution)/shard_map/reduce_scatter | solution.py:234
  382.3 961.3 %all-reduce.16.cloned.1.call-start = ((), (), s32[]{:S(2)}) async-start(), calls=%async_computation.23 | async-start | bytes 29818880 | tf_op jit(solution)/shard_map/psum | solution.py:236
  875.4 8.0 copy-start.16
  875.4 8.1 copy-start.21
  875.4 8.4 copy-start.19
  875.4 8.9 copy-start.38
  1343.6 12.1 copy-start.6
  1351.0 6.8 slice-start.4
  1355.8 2.1 slice-start.5
  (3 other events, 2.3 us)
Sparse Core Ops, SparseCore 0:
  9.7 23.8 all-gather.7
  35.1 21.2 all-gather.9
  58.0 60.1 all-gather.11
  119.6 60.1 all-gather.13
  181.2 60.2 all-gather.15
  294.1 21.6 reduce-scatter.9
  318.9 21.6 reduce-scatter.11
  343.7 21.1 reduce-scatter.15
  368.0 21.1 reduce-scatter.17
  392.2 38.3 reduce-scatter.13
  433.9 38.3 reduce-scatter.19
  474.8 130.0 reduce-scatter.21
  607.7 130.0 reduce-scatter.23
  740.4 130.0 reduce-scatter.25
  877.1 466.4 all-reduce.15
where the time goes:
time: 1380 us; the launch traced here: 1370 us
  waiting for transfers between devices  1090 us (79%)
  matrix products  138 us (10%)
  blocking collectives  68.8 us (5%)
  local copies, waits for them, and re-layouts  28.1 us (2%)
  other arithmetic  26.6 us (2%)
  between operations  17.8 us (1%)
    psum x1, waiting for transfers between devices, body(): shards = lax.psum(tuple(shards), 'replica')  424 us
    reduce_scatter x1, waiting for transfers between devices, body(): lax.psum_scatter(grad_up, 'group', scatter_dimension=0, tiled=True)  133 us
    reduce_scatter x1, waiting for transfers between devices, body(): lax.psum_scatter(grad_gate, 'group', scatter_dimension=0, tiled=True)  133 us
    reduce_scatter x1, waiting for transfers between devices, body(): lax.psum_scatter(grad_down, 'group', scatter_dimension=0, tiled=True)  133 us
    all_gather x1, waiting for transfers between devices, body(): lax.all_gather(w_down, 'group', axis=0, tiled=True)  53.8 us
    all_gather x1, waiting for transfers between devices, body(): lax.all_gather(w_up, 'group', axis=0, tiled=True)  53.7 us
    reduce_scatter x1, waiting for transfers between devices, body(): lax.psum_scatter(grad_wo, 'group', scatter_dimension=0, tiled=True)  41.7 us
    reduce_scatter x1, waiting for transfers between devices, body(): lax.psum_scatter(grad_wq, 'group', scatter_dimension=0, tiled=True)  41.4 us
  transfers between devices with their start and end apart: 15, of which 12 were waited for; matrix products, arithmetic and copies ran while one was open for 9% of the time, Pallas kernels for 0%

commit v1 on v0

--- a/solution.py
+++ b/solution.py
@@ -8,6 +8,22 @@
 HEAD_DIM = 64
 EPSILON = 1e-06
 THETA = 1000000.0
+
+
+def gather_around(x, axis, dim):
+    ways, here, step = (lax.axis_size(axis), lax.axis_index(axis), x.shape[dim])
+    dims = [n * ways if d == dim else n for d, n in enumerate(x.shape)]
+    full = lax.dynamic_update_slice_in_dim(jnp.zeros(dims, x.dtype), x, here * step, axis=dim)
+    going_up = going_down = x
+    for far in range(1, ways // 2 + 1):
+        going_up = lax.ppermute(going_up, axis, [(d, (d + 1) % ways) for d in range(ways)])
+        full = lax.dynamic_update_slice_in_dim(full, going_up, (here - far) % ways * step, axis=dim)
+        if 2 * far < ways:
+            going_down = lax.ppermute(going_down, axis, [(d, (d - 1) % ways) for d in range(ways)])
+            full = lax.dynamic_update_slice_in_dim(
+                full, going_down, (here + far) % ways * step, axis=dim
+            )
+    return full
 
 
 def rms_scale(values):
@@ -77,7 +93,7 @@
     )
     mlp_full = (
         lax.all_gather(gain_two, "group", axis=0, tiled=True),
-        lax.all_gather(w_gate, "group", axis=0, tiled=True),
+        gather_around(w_gate, "group", 0),
         lax.all_gather(w_up, "group", axis=0, tiled=True),
         lax.all_gather(w_down, "group", axis=0, tiled=True),
     )

time: 1380 us -> 1390 us (level)
  waiting for transfers between devices: 1090 us -> 1020 us
  blocking collectives: 68.8 us -> 132 us
  local copies, waits for them, and re-layouts: 28.1 us -> 43.5 us
    all_gather x1, blocking collectives: 6.9 us -> 67.2 us  [body(): lax.all_gather(w_value, 'group', axis=0, tiled=True)]
    all_gather x1, waiting for transfers between devices: 53.8 us -> 0.01 us  [body(): lax.all_gather(w_down, 'group', axis=0, tiled=True)]
    all_gather x1, waiting for transfers between devices: 53.7 us -> 26.5 us  [body(): lax.all_gather(w_up, 'group', axis=0, tiled=True)]
  transfers between devices with their start and end apart: 15 -> 18, of which waited for: 12 -> 12; matrix products, arithmetic and copies ran while one was open for 9% -> 11% of each run, Pallas kernels for 0% -> 0%
where the time goes in v1:
time: 1390 us; the launch traced here: 1380 us
  waiting for transfers between devices  1020 us (73%)
  matrix products  138 us (10%)
  blocking collectives  132 us (9%)
  local copies, waits for them, and re-layouts  43.5 us (3%)
  other arithmetic  25.7 us (2%)
  between operations  17.7 us (1%)
    psum x1, waiting for transfers between devices, body(): shards = lax.psum(tuple(shards), 'replica')  424 us
    reduce_scatter x1, waiting for transfers between devices, body(): lax.psum_scatter(grad_up, 'group', scatter_dimension=0, tiled=True)  133 us
    reduce_scatter x1, waiting for transfers between devices, body(): lax.psum_scatter(grad_down, 'group', scatter_dimension=0, tiled=True)  133 us
    reduce_scatter x1, waiting for transfers between devices, body(): lax.psum_scatter(grad_gate, 'group', scatter_dimension=0, tiled=True)  133 us
    all_gather x1, blocking collectives, body(): lax.all_gather(w_value, 'group', axis=0, tiled=True)  67.2 us
    all_gather x1, waiting for transfers between devices, body(): lax.all_gather(w_gate, 'group', axis=0, tiled=True)  45.8 us
    reduce_scatter x1, waiting for transfers between devices, body(): lax.psum_scatter(grad_wo, 'group', scatter_dimension=0, tiled=True)  41.7 us
    reduce_scatter x1, waiting for transfers between devices, body(): lax.psum_scatter(grad_wq, 'group', scatter_dimension=0, tiled=True)  41.4 us
  transfers between devices with their start and end apart: 18, of which 12 were waited for; matrix products, arithmetic and copies ran while one was open for 11% of the time, Pallas kernels for 0%

profile of v1, /device:TPU:0, one launch (start us, length us, event | category | flops | bytes accessed | tf_op | source)
XLA Modules:
  0.0 1382.8 jit_solution(14937500294804330096)
XLA Ops:
  10.6 2.0 collective-permute-start.1
  12.7 67.2 %all_gather.51 = bf16[896,128]{1,0:T(8,128)(2,1)S(1)} all-gather(bf16[224,128]{1,0:T(8,128)(2,1)S(1)} %copy-done.31), channel_id=1, replica_groups=mesh['group'=4,'replica'=8] {'group'}, dimensions={0}, use_global_device_ids=true | all-gather | bytes 286720 | tf_op jit(solution)/shard_map/all_gather | solution.py:90
  83.1 8.7 all-reduce.13
  92.2 6.9 all_gather.54
  99.8 7.7 all-gather
  109.1 7.6 all-gather.1
  117.0 3.9 broadcast_in_dim.22
  120.9 3.1 constant_dynamic-update-slice_fusion.3
  124.6 3.1 constant_dynamic-update-slice_fusion.2
  127.7 3.1 constant_dynamic-update-slice_fusion.1
  130.8 2.2 convolution_add_fusion.2
  133.6 7.4 fusion.5
  141.0 8.1 fusion.6
  149.2 10.0 fusion.22
  159.3 2.4 multiply_reduce_fusion
  161.9 5.8 collective-permute-done.2
  167.8 3.1 constant_dynamic-update-slice_fusion
  170.8 9.9 fusion.52
  180.8 26.5 %all-gather.12.cloned.1.call-done = bf16[896,4864]{1,0:T(8,128)(2,1)} async-done(((bf16[224,4864]{1,0:T(8,128)(2,1)}), bf16[896,4864]{1,0:T(8,128)(2,1)}) %all-gather.12.cloned.1.call-update) | async-done | bytes 8716304 | tf_op jit(solution)/shard_map/all_gather | solution.py:97
  207.2 5.4 fusion.86
  212.7 10.3 multiply_convert_fusion
  223.0 45.8 %all-gather.16.cloned.1.call-done = bf16[896,4864]{1,0:T(8,128)(2,1)} async-done(((bf16[224,4864]{1,0:T(8,128)(2,1)}), bf16[896,4864]{1,0:T(8,128)(2,1)}) %all-gather.16.cloned.1.call-update) | async-done | bytes 8716304 | tf_op jit(solution)/shard_map/all_gather | solution.py:153
  268.8 7.1 fusion.87
  276.3 3.5 fusion.39
  279.7 1.0 fusion.44
  281.7 12.5 fusion
  294.2 1.5 slice-done.2
  296.3 7.6 fusion.9
  303.9 2.9 copy-done
  306.8 3.1 fusion.25
  310.1 7.5 fusion.12
  318.4 13.4 reduce-scatter.10.cloned.1.call-done
  332.7 1.5 convert_reduce_fusion.2
  334.2 1.2 fusion.67
  335.8 5.4 broadcast_multiply_fusion
  341.1 15.6 %reduce-scatter.12.cloned.1.call-done = f32[1,256,128]{1,2,0:T(8,128)} async-done(((f32[1,1024,128]{1,2,0:T(8,128)}), f32[1,256,128]{1,2,0:T(8,128)}) %reduce-scatter.12.cloned.1.call-update) | async-done | bytes 131088 | tf_op jit(solution)/shard_map/reduce_scatter | solution.py:207
  356.7 2.1 fusion.64
  359.0 1.0 copy-done.3
  360.1 1.5 add_convert_fusion
  361.6 2.5 fusion.79
  364.1 2.3 fusion.47
  366.5 10.3 fusion.89
  376.8 10.1 fusion.90
  388.0 10.6 fusion.50
  398.9 6.5 reduce-scatter.18.cloned.1.call-done
  405.4 41.4 %reduce-scatter.14.cloned.1.call-done = f32[224,896]{1,0:T(8,128)} async-done(((f32[896,896]{1,0:T(8,128)}), f32[224,896]{1,0:T(8,128)}) %reduce-scatter.14.cloned.1.call-update) | async-done | bytes 802832 | tf_op jit(solution)/shard_map/reduce_scatter | solution.py:240
  446.7 41.7 %reduce-scatter.20.cloned.1.call-done = f32[224,896]{1,0:T(8,128)} async-done(((f32[896,896]{1,0:T(8,128)}), f32[224,896]{1,0:T(8,128)}) %reduce-scatter.20.cloned.1.call-update) | async-done | bytes 802832 | tf_op jit(solution)/shard_map/reduce_scatter | solution.py:246
  488.4 132.6 %reduce-scatter.22.cloned.1.call-done = f32[224,4864]{1,0:T(8,128)} async-done(((f32[896,4864]{1,0:T(8,128)}), f32[224,4864]{1,0:T(8,128)}) %reduce-scatter.22.cloned.1.call-update) | async-done | bytes 4358160 | tf_op jit(solution)/shard_map/reduce_scatter | solution.py:248
  621.1 132.9 %reduce-scatter.24.cloned.1.call-done = f32[224,4864]{1,0:T(8,128)} async-done(((f32[896,4864]{1,0:T(8,128)}), f32[224,4864]{1,0:T(8,128)}) %reduce-scatter.24.cloned.1.call-update) | async-done | bytes 4358160 | tf_op jit(solution)/shard_map/reduce_scatter | solution.py:249
  754.0 132.6 %reduce-scatter.26.cloned.1.call-done = f32[1216,896]{1,0:T(8,128)} async-done(((f32[4864,896]{1,0:T(8,128)}), f32[1216,896]{1,0:T(8,128)}) %reduce-scatter.26.cloned.1.call-update) | async-done | bytes 4358160 | tf_op jit(solution)/shard_map/reduce_scatter | solution.py:250
  888.0 1.3 fusion.41
  889.4 2.2 fusion.88
  891.6 8.0 fusion.21
  900.5 10.9 all-reduce.12
  911.8 23.2 %all-reduce.10 = (f32[224]{0:T(256)}, f32[224]{0:T(256)}, f32[32]{0:T(128)}, f32[32]{0:T(128)}, f32[224]{0:T(256)}) all-reduce(f32[224]{0:T(256)S(1)} %dynamic-slice.6, f32[224]{0:T(256)S(1)} %dynamic-slice.8, f32[32]{0:T(128)S(1)} %dynamic-slice.10, f32[32]{0:T(128)S(1)} %dynamic-slice.12, ...), channel_id=1, replica_groups=mesh['group'=4,'replica'=8] {'replica'}, use_global_device_ids=true, to_apply=%region_11.12 | all-reduce | flops 736 | bytes 5888 | tf_op jit(solution)/shard_map/psum | solution.py:252
  935.0 1.1 fusion.32
  936.1 423.7 %all-reduce.16.cloned.1.call-done = (f32[224,896]{1,0:T(8,128)}, f32[224,128]{1,0:T(8,128)}, f32[224,128]{1,0:T(8,128)}, f32[224,896]{1,0:T(8,128)}, f32[224,486...) async-done(((f32[224,896]{1,0:T(8,128)}, f32[224,128]{1,0:T(8,128)}, f32[224,128]{1,0:T(8,128)}, f32[224,896]{1,0:T(8,128)}, f32[224,4864]{1,0:T(8,128)}, ...) | async-done | bytes 14909456 | tf_op jit(solution)/shard_map/psum | solution.py:252
  1359.7 2.2 copy.81
  1362.0 1.6 copy.82
  1363.5 1.6 copy.83
  1365.1 2.1 copy.84
  1367.2 4.7 copy.85
  1371.9 2.1 copy.86
  1374.0 2.1 copy.87
  (203 shorter events, 16.5 us)
Async XLA Ops:
  7.2 72.8 %copy-start.41 = (u32[32]{0:T(128)S(1)}, u32[32]{0:T(128)}, u32[]{:S(2)}) copy-start(u32[32]{0:T(128)} %constant.75) | copy-start | bytes 388
  7.2 5.5 copy-start.31
  7.2 74.7 %copy-start.44 = (bf16[32]{0:T(256)(128)(2,1)S(1)}, bf16[32]{0:T(256)(128)(2,1)}, u32[]{:S(2)}) copy-start(bf16[32]{0:T(256)(128)(2,1)} %param.26) | copy-start | bytes 196
  7.2 75.0 %copy-start.45 = (bf16[32]{0:T(256)(128)(2,1)S(1)}, bf16[32]{0:T(256)(128)(2,1)}, u32[]{:S(2)}) copy-start(bf16[32]{0:T(256)(128)(2,1)} %param.24) | copy-start | bytes 196
  7.2 75.2 %copy-start.46 = (bf16[224]{0:T(256)(128)(2,1)S(1)}, bf16[224]{0:T(256)(128)(2,1)}, u32[]{:S(2)}) copy-start(bf16[224]{0:T(256)(128)(2,1)} %param.20) | copy-start | bytes 1348
  7.2 75.4 %copy-start.47 = (bf16[224]{0:T(256)(128)(2,1)S(1)}, bf16[224]{0:T(256)(128)(2,1)}, u32[]{:S(2)}) copy-start(bf16[224]{0:T(256)(128)(2,1)} %param.22) | copy-start | bytes 1348
  7.2 75.7 %copy-start.48 = (bf16[224]{0:T(256)(128)(2,1)S(1)}, bf16[224]{0:T(256)(128)(2,1)}, u32[]{:S(2)}) copy-start(bf16[224]{0:T(256)(128)(2,1)} %param.28) | copy-start | bytes 1348
  7.3 84.6 %copy-start.1 = (bf16[1,256,896]{2,1,0:T(8,128)(2,1)S(1)}, bf16[1,256,896]{2,1,0:T(8,128)(2,1)}, u32[]{:S(2)}) copy-start(bf16[1,256,896]{2,1,0:T(8,128)(2,1)} %param.16) | copy-start | bytes 1376260
  7.3 84.8 %copy-start.43 = (s32[1,256]{1,0:T(1,128)S(1)}, s32[1,256]{1,0:T(1,128)}, u32[]{:S(2)}) copy-start(s32[1,256]{1,0:T(1,128)} %param.18) | copy-start | bytes 3076
  7.3 84.9 %copy-start.32 = (bf16[224,128]{1,0:T(8,128)(2,1)S(1)}, bf16[224,128]{1,0:T(8,128)(2,1)}, u32[]{:S(2)}) copy-start(bf16[224,128]{1,0:T(8,128)(2,1)} %param.23) | copy-start | bytes 172036
  7.3 109.5 %copy-start.39 = (s32[1,1024]{1,0:T(1,128)S(1)}, s32[1,1024]{1,0:T(1,128)}, u32[]{:S(2)}) copy-start(s32[1,1024]{1,0:T(1,128)} %param.19) | copy-start | bytes 12292
  7.3 123.5 %all-gather.8.cloned.1.call-start = ((), (), s32[]{:S(2)}) async-start(), calls=%async_computation.9 | async-start | bytes 2007040 | tf_op jit(solution)/shard_map/all_gather | solution.py:86
  8.0 151.2 %all-gather.10.cloned.1.call-start = ((), (), s32[]{:S(2)}) async-start(), calls=%async_computation.10 | async-start | bytes 2007040 | tf_op jit(solution)/shard_map/all_gather | solution.py:92
  8.8 162.0 %all-gather.14.cloned.1.call-start = ((), (), s32[]{:S(2)}) async-start(), calls=%async_computation.12 | async-start | bytes 10895360 | tf_op jit(solution)/shard_map/all_gather | solution.py:98
  9.5 197.7 %all-gather.12.cloned.1.call-start = ((), (), s32[]{:S(2)}) async-start(), calls=%async_computation.11 | async-start | bytes 10895360 | tf_op jit(solution)/shard_map/all_gather | solution.py:97
  10.1 258.7 %all-gather.16.cloned.1.call-start = ((), (), s32[]{:S(2)}) async-start(), calls=%async_computation.13 | async-start | bytes 10895360 | tf_op jit(solution)/shard_map/all_gather | solution.py:153
  10.1 113.8 %collective-permute-start = (bf16[224,4864]{1,0:T(8,128)(2,1)}, bf16[224,4864]{1,0:T(8,128)(2,1)}, u32[]{:S(2)}, u32[]{:S(2)}) collective-permute-start(bf16[224,4864]{1,0:T(8,128)(2,1)} %param.29), channel_id=1, source_target_pairs={{0,8},{8,16},{16,24},{24,0},{1,9},{9,17},{17,25},{25,1},{2,10},{10... | collective-permute-start | bytes 6537224 | tf_op jit(solution)/shard_map/ppermute | solution.py:19
  10.6 117.1 %collective-permute-start.1 = (bf16[224,4864]{1,0:T(8,128)(2,1)}, bf16[224,4864]{1,0:T(8,128)(2,1)}, u32[]{:S(2)}, u32[]{:S(2)}) collective-permute-start(bf16[224,4864]{1,0:T(8,128)(2,1)} %param.29), channel_id=1, source_target_pairs={{0,24},{8,0},{16,8},{24,16},{1,25},{9,1},{17,9},{25,17},{2,26},{10... | collective-permute-start | bytes 6537224 | tf_op jit(solution)/shard_map/ppermute | solution.py:22
  12.7 319.1 %reduce-scatter.10.cloned.1.call-start = ((), (), s32[]{:S(2)}) async-start(), calls=%async_computation.14 | async-start | bytes 655360 | tf_op jit(solution)/shard_map/reduce_scatter | solution.py:201
  80.0 19.4 %copy-start.19 = (bf16[896,128]{1,0:T(8,128)(2,1)}, bf16[896,128]{1,0:T(8,128)(2,1)S(1)}, u32[]{:S(2)}) copy-start(bf16[896,128]{1,0:T(8,128)(2,1)S(1)} %all_gather.51) | copy-start | bytes 688132
  91.8 39.0 %copy-start.28 = (f32[896]{0:T(1024)}, f32[896]{0:T(1024)S(1)}, u32[]{:S(2)}) copy-start(f32[896]{0:T(1024)S(1)} %convert_element_type.154) | copy-start | bytes 10756
  92.1 16.9 %copy-start.25 = (f32[1,256,32]{1,2,0:T(8,128)}, f32[1,256,32]{1,2,0:T(8,128)S(1)}, u32[]{:S(2)}) copy-start(f32[1,256,32]{1,2,0:T(8,128)S(1)} %broadcast_multiply_fusion.2) | copy-start | bytes 98308
  92.1 38.7 %copy-start.35 = (f32[256]{0:T(256)}, f32[256]{0:T(256)S(1)}, u32[]{:S(2)}) copy-start(f32[256]{0:T(256)S(1)} %add_rsqrt_fusion.1) | copy-start | bytes 3076
  116.8 16.8 %copy-start.8 = (bf16[1024,128]{0,1:T(8,128)(2,1)}, bf16[1024,128]{0,1:T(8,128)(2,1)S(1)}, u32[]{:S(2)}) copy-start(bf16[1024,128]{0,1:T(8,128)(2,1)S(1)} %all-gather.1) | copy-start | bytes 786436
  123.9 43.8 %collective-permute-start.2 = (bf16[224,4864]{1,0:T(8,128)(2,1)}, bf16[224,4864]{1,0:T(8,128)(2,1)}, u32[]{:S(2)}, u32[]{:S(2)}) collective-permute-start(bf16[224,4864]{1,0:T(8,128)(2,1)} %collective-permute-done), channel_id=1, source_target_pairs={{0,8},{8,16},{16,24},{24,0},{1,9},{9,17},{17,25},{25,1},{2,10},{10... | collective-permute-start | bytes 6537224 | tf_op jit(solution)/shard_map/ppermute | solution.py:19
  141.0 8.1 copy-start.16
  149.1 12.6 copy-start.33
  159.2 11.6 copy-start.12
  161.7 118.0 %copy-start.4 = (f32[1,256,896]{2,1,0:T(8,128)}, f32[1,256,896]{2,1,0:T(8,128)S(1)}, u32[]{:S(2)}) copy-start(f32[1,256,896]{2,1,0:T(8,128)S(1)} %get-tuple-element.64) | copy-start | bytes 2752516
  161.7 114.3 %copy-start.38 = (f32[256]{0:T(256)}, f32[256]{0:T(256)S(1)}, u32[]{:S(2)}) copy-start(f32[256]{0:T(256)S(1)} %add_rsqrt_fusion) | copy-start | bytes 3076
  207.2 5.4 copy-start.49
  268.8 7.1 copy-start.2
  268.8 7.4 copy-start.7
  281.7 12.5 slice-start
  281.7 12.5 slice-start.1
  281.7 14.0 %slice-start.2 = ((s8[14680064]{0:T(1024)(128)(4,1)}), s8[4194304]{0:T(1024)(128)(4,1)S(1)}, s32[]{:S(2)}) async-start(s8[14680064]{0:T(1024)(128)(4,1)} %bitcast.257), calls=%async_computation.26 | async-start | bytes 8388608
  281.7 14.6 %slice-start.3 = ((s8[14680064]{0:T(1024)(128)(4,1)}), s8[2097152]{0:T(1024)(128)(4,1)S(1)}, s32[]{:S(2)}) async-start(s8[14680064]{0:T(1024)(128)(4,1)} %bitcast.257), calls=%async_computation.27 | async-start | bytes 4194304
  310.0 7.7 copy-start.26
  310.0 24.2 %copy-start.29 = (f32[896]{0:T(1024)S(1)}, f32[896]{0:T(1024)}, u32[]{:S(2)}) copy-start(f32[896]{0:T(1024)} %copy-done.28) | copy-start | bytes 10756
  310.0 24.2 %copy-start.36 = (f32[256]{0:T(256)S(1)}, f32[256]{0:T(256)}, u32[]{:S(2)}) copy-start(f32[256]{0:T(256)} %copy-done.35) | copy-start | bytes 3076
  310.0 25.7 %copy-start.9 = (bf16[1024,128]{0,1:T(8,128)(2,1)S(1)}, bf16[1024,128]{0,1:T(8,128)(2,1)}, u32[]{:S(2)}) copy-start(bf16[1024,128]{0,1:T(8,128)(2,1)} %copy-done.8) | copy-start | bytes 786436
  310.0 46.7 %reduce-scatter.12.cloned.1.call-start = ((), (), s32[]{:S(2)}) async-start(), calls=%async_computation.15 | async-start | bytes 655360 | tf_op jit(solution)/shard_map/reduce_scatter | solution.py:207
  317.6 81.3 %reduce-scatter.16.cloned.1.call-start = ((), (), s32[]{:S(2)}) async-start(), calls=%async_computation.17 | async-start | bytes 573440 | tf_op jit(solution)/shard_map/reduce_scatter | solution.py:242
  318.4 40.6 %copy-start.17 = (f32[256,64]{0,1:T(8,128)}, f32[256,64]{0,1:T(8,128)S(1)}, u32[]{:S(2)}) copy-start(f32[256,64]{0,1:T(8,128)S(1)} %get-tuple-element.56) | copy-start | bytes 196612
  334.2 24.8 %copy-start.23 = (bf16[1,256,128]{1,2,0:T(8,128)(2,1)}, bf16[1,256,128]{1,2,0:T(8,128)(2,1)S(1)}, u32[]{:S(2)}) copy-start(bf16[1,256,128]{1,2,0:T(8,128)(2,1)S(1)} %get-tuple-element.41) | copy-start | bytes 196612
  335.4 24.6 %copy-start.27 = (f32[256,64]{0,1:T(8,128)S(1)}, f32[256,64]{0,1:T(8,128)}, u32[]{:S(2)}) copy-start(f32[256,64]{0,1:T(8,128)} %get-tuple-element.55) | copy-start | bytes 196612
  335.5 26.1 %copy-start.30 = (f32[896]{0:T(1024)S(1)}, f32[896]{0:T(1024)}, u32[]{:S(2)}) copy-start(f32[896]{0:T(1024)} %copy-done.28) | copy-start | bytes 10756
  335.5 26.1 %copy-start.37 = (f32[256]{0:T(256)S(1)}, f32[256]{0:T(256)}, u32[]{:S(2)}) copy-start(f32[256]{0:T(256)} %copy-done.35) | copy-start | bytes 3076
  335.5 69.9 %reduce-scatter.18.cloned.1.call-start = ((), (), s32[]{:S(2)}) async-start(), calls=%async_computation.18 | async-start | bytes 573440 | tf_op jit(solution)/shard_map/reduce_scatter | solution.py:244
  358.8 5.3 copy-start.11
  358.8 87.9 %reduce-scatter.14.cloned.1.call-start = ((), (), s32[]{:S(2)}) async-start(), calls=%async_computation.16 | async-start | bytes 4014080 | tf_op jit(solution)/shard_map/reduce_scatter | solution.py:240
  364.0 124.4 %reduce-scatter.20.cloned.1.call-start = ((), (), s32[]{:S(2)}) async-start(), calls=%async_computation.19 | async-start | bytes 4014080 | tf_op jit(solution)/shard_map/reduce_scatter | solution.py:246
  366.5 254.6 %reduce-scatter.22.cloned.1.call-start = ((), (), s32[]{:S(2)}) async-start(), calls=%async_computation.20 | async-start | bytes 21790720 | tf_op jit(solution)/shard_map/reduce_scatter | solution.py:248
  376.8 377.2 %reduce-scatter.24.cloned.1.call-start = ((), (), s32[]{:S(2)}) async-start(), calls=%async_computation.21 | async-start | bytes 21790720 | tf_op jit(solution)/shard_map/reduce_scatter | solution.py:249
  387.0 499.6 %reduce-scatter.26.cloned.1.call-start = ((), (), s32[]{:S(2)}) async-start(), calls=%async_computation.22 | async-start | bytes 21790720 | tf_op jit(solution)/shard_map/reduce_scatter | solution.py:250
  398.6 961.1 %all-reduce.16.cloned.1.call-start = ((), (), s32[]{:S(2)}) async-start(), calls=%async_computation.23 | async-start | bytes 29818880 | tf_op jit(solution)/shard_map/psum | solution.py:252
  891.5 8.0 copy-start.15
  891.5 8.1 copy-start.22
  891.5 8.1 copy-start.24
  891.6 8.5 copy-start.20
  891.6 9.0 copy-start.40
  891.6 9.0 copy-start.42
  1359.7 12.1 copy-start.6
  1367.1 6.8 slice-start.4
  (10 other events, 23.1 us)
Sparse Core Ops, SparseCore 0:
  9.7 31.2 all-gather.7
  42.5 28.5 all-gather.9
  72.7 68.5 all-gather.13
  142.7 64.4 all-gather.11
  208.6 60.1 all-gather.15
  310.1 21.6 reduce-scatter.9
  335.0 21.6 reduce-scatter.11
  359.8 21.1 reduce-scatter.15
  384.1 21.1 reduce-scatter.17
  408.4 38.3 reduce-scatter.13
  450.0 38.3 reduce-scatter.19
  490.9 130.0 reduce-scatter.21
  623.9 130.0 reduce-scatter.23
  756.5 130.0 reduce-scatter.25
  893.2 466.4 all-reduce.15
